TPU v7x, 512 devices: a whole 4x4x16 slice. The times are simulated.
512 devices in a mesh: leaf: 128 (over z, y, core), rep: 4 (over x).
Axes of the slice: x: 4, y: 4, z: 16, core: 2. Of those that a mesh axis runs over, the one named last changes fastest.
Arguments:
- positions: float32 [3, 8192, 128], P(None, ('leaf', 'rep')), may hold values from -6 to 6
- density: float32 [3, 8192, 128], P(None, ('leaf', 'rep')), may hold values from -6 to 6
- near_offset: int32 [8192, 12], P(('leaf', 'rep')), may hold values from -2 to 2
- near_count: int32 [8192], P(('leaf', 'rep')), may hold values from 1 to 12
- inter_list: int32 [512, 189], P(('leaf', 'rep')), may hold values from 0 to 511
- operator_index: int32 [512, 189], P(('leaf', 'rep')), may hold values from 0 to 3
- lattice_index: int32 [512], P(('leaf', 'rep')), may hold values from 0 to 1
- up_weight: bfloat16 [512, 384], replicated, may hold values from -0.3125 to 0.3125
- m2l_operators: bfloat16 [4, 512, 512], replicated, may hold values from -0.0390625 to 0.0390625
- lattice_operators: bfloat16 [2, 512, 512], replicated, may hold values from -0.01171875 to 0.01171875
- down_weight: bfloat16 [384, 512], replicated, may hold values from -0.5 to 0.5
Outputs:
- velocity: float32 [3, 8192, 128], P(None, ('leaf', 'rep'))
Inputs may be any that keep to these rules, and one draw needn't show every extreme that they name: `near_offset`: leaf g's near source leaves are (g + offset) mod 8192; slots at or past near_count are unused.
All inputs are finite; a program needn't handle non-finite values.
Results may differ from a plain program's by a relative error of at most 0.02.
Values may be sent and summed in bfloat16 or wider, within the bound.
A program may use at most 64 MiB of HBM per device.

v0:
```python
import math
import jax
import jax.numpy as jnp
from jax import lax
from jax.sharding import PartitionSpec as P


def padded(shard, sides, width):
    for axis, dim in sides:
        size, length = (lax.axis_size(axis), shard.shape[dim])
        up = [(i, (i + 1) % size) for i in range(size)]
        down = [(j, i) for i, j in up]
        last = lax.slice_in_dim(shard, length - width, length, axis=dim)
        first = lax.slice_in_dim(shard, 0, width, axis=dim)
        before = lax.ppermute(last, axis, up)
        after = lax.ppermute(first, axis, down)
        shard = jnp.concatenate([before, shard, after], axis=dim)
    return shard


def stokes_tile(target, source_pos, source_force, live_slots):
    offsets_xyz = target[:, None, :, None] - source_pos[:, :, None, :]
    distance_sq = jnp.sum(offsets_xyz * offsets_xyz, axis=0) + 0.05
    inverse = lax.rsqrt(distance_sq)
    inverse_cube = inverse * inverse * inverse
    projected = jnp.sum(offsets_xyz * source_force[:, :, None, :], axis=0)
    kernel_terms = source_force[:, :, None, :] * inverse + offsets_xyz * (projected * inverse_cube)
    kernel_terms = kernel_terms * live_slots[None, :, None, None]
    return jnp.sum(kernel_terms, axis=(1, 3)) * (1.0 / (8.0 * math.pi))


def body(
    positions,
    density,
    near_offset,
    near_count,
    inter_list,
    operator_index,
    lattice_index,
    up_weight,
    m2l_operators,
    lattice_operators,
    down_weight,
):
    per_box = positions.shape[1]
    node_count = positions.shape[2]
    kind_count = m2l_operators.shape[0]
    stacked = jnp.concatenate([positions, density], axis=0)
    extended = padded(stacked.astype(jnp.bfloat16), ((("leaf", "rep"), 1),), per_box).astype(
        stacked.dtype
    )
    slot_range = jnp.arange(near_offset.shape[1], dtype=jnp.int32)

    def one_leaf(leaf_slot):
        target = positions[:, leaf_slot]
        source_slot = leaf_slot + near_offset[leaf_slot] + per_box
        sources = jnp.take(extended, source_slot, axis=1)
        live_slots = (slot_range < near_count[leaf_slot]).astype(jnp.float32)
        return stokes_tile(target, sources[:3], sources[3:], live_slots)

    near_part = lax.map(one_leaf, jnp.arange(per_box, dtype=jnp.int32))
    near_part = jnp.transpose(near_part, (1, 0, 2))
    damping = 1.0 / (1.0 + jnp.sum(positions * positions, axis=0))
    summed = jnp.sum(density * damping[None], axis=1).reshape(-1).astype(jnp.bfloat16)
    coarse = jnp.dot(up_weight, summed, preferred_element_type=jnp.float32).astype(jnp.bfloat16)
    coarse_row = coarse.reshape(1, -1)
    box_ids = inter_list[0]
    op_kinds = operator_index[0]
    kind_range = jnp.arange(kind_count, dtype=jnp.int32)
    selector = (op_kinds[None, :] == kind_range[:, None]).astype(jnp.float32)
    all_blocks = lax.all_gather(coarse_row, ("leaf", "rep"), axis=0, tiled=True)
    chosen = jnp.take(all_blocks, box_ids, axis=0).astype(jnp.float32)
    grouped_sum = jnp.dot(selector, chosen, precision=lax.Precision.HIGHEST)
    block_sum = jnp.sum(all_blocks.astype(jnp.float32), axis=0)
    block_sum = lax.psum(coarse.astype(jnp.float32), ("leaf", "rep"))
    total = block_sum.astype(jnp.bfloat16)
    grouped = grouped_sum.astype(jnp.bfloat16)
    local = jnp.einsum("tij,tj->i", m2l_operators, grouped, preferred_element_type=jnp.float32)
    local = local + jnp.dot(
        lattice_operators[lattice_index[0]], total, preferred_element_type=jnp.float32
    )
    local_bf = local.astype(jnp.bfloat16)
    far_part = jnp.dot(down_weight, local_bf, preferred_element_type=jnp.float32).reshape(
        3, node_count
    )
    return near_part + damping[None] * far_part[:, None, :]


def solution(mesh):
    in_specs = (
        P(None, ("leaf", "rep"), None),
        P(None, ("leaf", "rep"), None),
        P(("leaf", "rep"), None),
        P(("leaf", "rep")),
        P(("leaf", "rep"), None),
        P(("leaf", "rep"), None),
        P(("leaf", "rep")),
        P(),
        P(),
        P(),
        P(),
    )
    out_specs = P(None, ("leaf", "rep"), None)
    return jax.shard_map(body, mesh=mesh, in_specs=in_specs, out_specs=out_specs, check_vma=False)
```

profile of v0, /device:TPU:4, one launch (start us, length us, event | category | flops | bytes accessed | tf_op | source)
XLA Modules:
  0.0 417.0 jit_solution(9846070013614672958)
XLA Ops:
  1.8 3.1 collective-permute-start
  4.9 2.7 collective-permute-start.1
  8.9 108.3 %psum.7 = bf16[512]{0:T(512)(128)(2,1)S(1)} all-reduce(bf16[512]{0:T(512)(128)(2,1)S(1)} %convert_element_type.40), channel_id=1, replica_groups=mesh['leaf'=128,'rep'=4] {'leaf','rep'}, use_global_device_ids=true, to_apply=%region_7.8 | all-reduce | flops 512 | bytes 2048 | tf_op jit(solution)/shard_map/psum | solution.py:75
  117.8 136.1 %all-gather.1 = bf16[512,1,512]{2,1,0:T(2,128)(2,1)S(1)} all-gather(bf16[1,1,512]{2,1,0:T(2,128)(2,1)S(1)} %reshape.142), channel_id=2, replica_groups=mesh['leaf'=128,'rep'=4] {'leaf','rep'}, dimensions={0}, use_global_device_ids=true | all-gather | bytes 525312 | tf_op jit(solution)/shard_map/all_gather | solution.py:71
  257.8 158.6 %while.13 = (s32[]{:T(128)}, f32[16,3,128]{2,0,1:T(8,128)S(1)}, s32[16]{0:T(128)S(1)}, s32[16,12]{1,0:T(8,128)}, f32[6,48,128]{2,0,1:T(8,128)S(1)}, /*index=5*/f...) while((s32[]{:T(128)}, f32[16,3,128]{2,0,1:T(8,128)S(1)}, ...), condition=%wide.region_4.5_spmd.clone, body=%wide.region_0.4_spmd.clone.sunk | while | flops 6891705 | bytes 6684707 | solution.py:61
  260.5 1.4 fusion.33
  262.5 1.4 compare_and_fusion.3
  270.4 1.4 fusion.33
  272.4 1.4 compare_and_fusion.3
  282.3 1.4 compare_and_fusion.3
  292.2 1.4 compare_and_fusion.3
  302.1 1.4 compare_and_fusion.3
  312.0 1.4 compare_and_fusion.3
  322.0 1.4 compare_and_fusion.3
  331.9 1.4 compare_and_fusion.3
  341.8 1.4 compare_and_fusion.3
  349.7 1.4 fusion.33
  351.7 1.4 compare_and_fusion.3
  361.6 1.4 compare_and_fusion.3
  371.5 1.4 compare_and_fusion.3
  381.4 1.4 compare_and_fusion.3
  391.3 1.4 compare_and_fusion.3
  401.3 1.4 compare_and_fusion.3
  411.2 1.4 compare_and_fusion.3
  (322 shorter events, 104.7 us)
Async XLA Ops:
  0.0 255.4 %copy-start = (bf16[4,512,512]{2,1,0:T(8,128)(2,1)S(1)}, bf16[4,512,512]{2,1,0:T(8,128)(2,1)}, u32[]{:S(2)}) copy-start(bf16[4,512,512]{2,1,0:T(8,128)(2,1)} %param.21) | copy-start | bytes 6291460
  0.0 254.1 %copy-start.2 = (s32[1,189]{1,0:T(1,128)S(1)}, s32[1,189]{1,0:T(1,128)}, u32[]{:S(2)}) copy-start(s32[1,189]{1,0:T(1,128)} %param.17) | copy-start | bytes 2272
  1.8 255.9 %collective-permute-start = (bf16[6,16,128]{2,1,0:T(8,128)(2,1)S(1)}, bf16[6,16,128]{2,1,0:T(8,128)(2,1)S(1)}, u32[]{:S(2)}, u32[]{:S(2)}) collective-permute-start(bf16[6,16,128]{2,1,0:T(8,128)(2,1)S(1)} %pad_maximum_fusion), channel_id=1, source_target_pairs={{0,1},{1,2},{2,3},{3,4},{4,5},{5,6},{6,7},{7,8},{8,9},{9,10},{10,1... | collective-permute-start | bytes 73736 | tf_op jit(solution)/shard_map/ppermute | solution.py:15
  4.9 252.8 %collective-permute-start.1 = (bf16[6,16,128]{2,1,0:T(8,128)(2,1)S(1)}, bf16[6,16,128]{2,1,0:T(8,128)(2,1)S(1)}, u32[]{:S(2)}, u32[]{:S(2)}) collective-permute-start(bf16[6,16,128]{2,1,0:T(8,128)(2,1)S(1)} %pad_maximum_fusion), channel_id=1, source_target_pairs={{1,0},{2,1},{3,2},{4,3},{5,4},{6,5},{7,6},{8,7},{9,8},{10,9},{11,1... | collective-permute-start | bytes 73736 | tf_op jit(solution)/shard_map/ppermute | solution.py:16
  117.8 137.4 %copy-start.3 = (s32[1,189]{1,0:T(1,128)S(1)}, s32[1,189]{1,0:T(1,128)}, u32[]{:S(2)}) copy-start(s32[1,189]{1,0:T(1,128)} %param.18) | copy-start | bytes 2272
  254.1 3.2 copy-start.1
  255.2 2.6 copy-start.4
where the time goes:
time: 420 us; the launch traced here: 417 us
  blocking collectives  244 us (58%)
  other arithmetic  83.3 us (20%)
  local copies, waits for them, and re-layouts  44.2 us (11%)
  loops' own time  34.7 us (8%)
  starting transfers between devices  5.84 us (1%)
    all_gather x1, blocking collectives, body(): all_blocks = lax.all_gather(coarse_row, ('leaf', 'rep'), axis=0, tiled=True)  136 us
    psum x1, blocking collectives, body(): block_sum = lax.psum(coarse.astype(jnp.float32), ('leaf', 'rep'))  108 us
    another operation x1, loops' own time, body(): near_part = lax.map(one_leaf, jnp.arange(per_box, dtype=jnp.int32))  34.7 us
    select_n x32, other arithmetic, one_leaf(): sources = jnp.take(extended, source_slot, axis=1)  23.5 us
    and x16, other arithmetic, one_leaf(): sources = jnp.take(extended, source_slot, axis=1)  22.2 us
    dynamic_slice x32, local copies, waits for them, and re-layouts, one_leaf(): target = positions[:, leaf_slot]  11.6 us
    convert_element_type x16, other arithmetic, one_leaf(): live_slots = (slot_range < near_count[leaf_slot]).astype(jnp.float32)  11 us
    reduce_sum x16, other arithmetic, stokes_tile(): return jnp.sum(kernel_terms, axis=(1, 3)) * (1.0 / (8.0 * math.pi))  10.7 us
  transfers between devices with their start and end apart: 2, of which 0 were waited for; matrix products, arithmetic and copies ran while one was open for 1% of the time, Pallas kernels for 0%

commit v1 on v0

--- a/solution.py
+++ b/solution.py
@@ -1,8 +1,21 @@
+import functools
 import math
 import jax
 import jax.numpy as jnp
 from jax import lax
 from jax.sharding import PartitionSpec as P
+
+
+def blocks_plan(view, dim_k):
+    return jnp.concatenate(
+        lax.all_to_all(
+            jnp.stack([view for _ in range(lax.axis_size(("leaf", "rep")))]), ("leaf", "rep"), 0, 0
+        ),
+        dim_k,
+    )
+
+
+bind_heaps = functools.partial(blocks_plan, dim_k=0)
 
 
 def padded(shard, sides, width):
@@ -68,7 +81,7 @@
     op_kinds = operator_index[0]
     kind_range = jnp.arange(kind_count, dtype=jnp.int32)
     selector = (op_kinds[None, :] == kind_range[:, None]).astype(jnp.float32)
-    all_blocks = lax.all_gather(coarse_row, ("leaf", "rep"), axis=0, tiled=True)
+    all_blocks = bind_heaps(coarse_row)
     chosen = jnp.take(all_blocks, box_ids, axis=0).astype(jnp.float32)
     grouped_sum = jnp.dot(selector, chosen, precision=lax.Precision.HIGHEST)
     block_sum = jnp.sum(all_blocks.astype(jnp.float32), axis=0)

time: 420 us -> 320 us (0.76)
  the two profiles are of different devices: /device:TPU:4 before, /device:TPU:1 now
where the time goes in v1:
time: 320 us; the launch traced here: 317 us
  blocking collectives  109 us (34%)
  other arithmetic  88.2 us (28%)
  local copies, waits for them, and re-layouts  50.3 us (16%)
  loops' own time  34.8 us (11%)
  starting transfers between devices  30.2 us (9%)
  matrix products  3.58 us (1%)
    psum x1, blocking collectives, body(): block_sum = lax.psum(coarse.astype(jnp.float32), ('leaf', 'rep'))  109 us
    another operation x1, loops' own time, body(): near_part = lax.map(one_leaf, jnp.arange(per_box, dtype=jnp.int32))  34.8 us
    select_n x32, other arithmetic, one_leaf(): sources = jnp.take(extended, source_slot, axis=1)  23.5 us
    all_to_all x1, starting transfers between devices, blocks_plan(): lax.all_to_all(jnp.stack([view for _ in range(lax.axis_size(('leaf', 'rep...  22.5 us
    and x16, other arithmetic, one_leaf(): sources = jnp.take(extended, source_slot, axis=1)  22.3 us
    dynamic_slice x32, local copies, waits for them, and re-layouts, one_leaf(): target = positions[:, leaf_slot]  11.6 us
    convert_element_type x16, other arithmetic, one_leaf(): live_slots = (slot_range < near_count[leaf_slot]).astype(jnp.float32)  11.1 us
    reduce_sum x16, other arithmetic, stokes_tile(): return jnp.sum(kernel_terms, axis=(1, 3)) * (1.0 / (8.0 * math.pi))  11 us
  transfers between devices with their start and end apart: 3, of which 0 were waited for; matrix products, arithmetic and copies ran while one was open for 42% of the time, Pallas kernels for 0%

profile of v1, /device:TPU:1, one launch (start us, length us, event | category | flops | bytes accessed | tf_op | source)
XLA Modules:
  0.0 316.6 jit_solution(16698145227748254225)
XLA Ops:
  1.8 3.9 %collective-permute-start = (bf16[6,16,128]{2,1,0:T(8,128)(2,1)S(1)}, bf16[6,16,128]{2,1,0:T(8,128)(2,1)S(1)}, u32[]{:S(2)}, u32[]{:S(2)}) collective-permute-start(bf16[6,16,128]{2,1,0:T(8,128)(2,1)S(1)} %pad_maximum_fusion), channel_id=1, source_target_pairs={{0,1},{1,2},{2,3},{3,4},{4,5},{5,6},{6,7},{7,8},{8,9},{9,10},{10,1... | collective-permute-start | bytes 73736 | tf_op jit(solution)/shard_map/ppermute | solution.py:28
  5.7 3.7 %collective-permute-start.1 = (bf16[6,16,128]{2,1,0:T(8,128)(2,1)S(1)}, bf16[6,16,128]{2,1,0:T(8,128)(2,1)S(1)}, u32[]{:S(2)}, u32[]{:S(2)}) collective-permute-start(bf16[6,16,128]{2,1,0:T(8,128)(2,1)S(1)} %pad_maximum_fusion), channel_id=1, source_target_pairs={{1,0},{2,1},{3,2},{4,3},{5,4},{6,5},{7,6},{8,7},{9,8},{10,9},{11,1... | collective-permute-start | bytes 73736 | tf_op jit(solution)/shard_map/ppermute | solution.py:29
  11.8 4.6 %reduce.2 = bf16[512,512]{1,0:T(8,128)(2,1)} reduce(bf16[512,1,512]{2,1,0:T(2,128)(2,1)S(1)} %stack.3, bf16[]{:T(256)} %broadcast.198), dimensions={1}, to_apply=%stack.3.reduce_sub_computation | reduce | bytes 1048578 | tf_op jit(solution)/shard_map/stack | solution.py:12
  16.4 2.0 reshape.156
  18.4 22.5 %all-to-all-start = ((bf16[512,2,256]{2,1,0:T(2,128)(2,1)}), bf16[512,2,256]{2,1,0:T(2,128)(2,1)S(1)}, u32[]{:S(2)}, u32[]{:S(2)}) async-start(bf16[512,2,256]{2,1,0:T(2,128)(2,1)} %reshape.156), calls=%async_computation | async-start | bytes 1048576 | tf_op jit(solution)/shard_map/all_to_all | solution.py:11
  40.9 108.7 %psum.7 = bf16[512]{0:T(512)(128)(2,1)S(1)} all-reduce(bf16[512]{0:T(512)(128)(2,1)S(1)} %convert_element_type.40), channel_id=1, replica_groups=mesh['leaf'=128,'rep'=4] {'leaf','rep'}, use_global_device_ids=true, to_apply=%region_7.8 | all-reduce | flops 512 | bytes 2048 | tf_op jit(solution)/shard_map/psum | solution.py:88
  151.7 159.0 %while.13 = (s32[]{:T(128)}, f32[16,3,128]{2,0,1:T(8,128)S(1)}, s32[16]{0:T(128)S(1)}, s32[16,12]{1,0:T(8,128)}, f32[6,48,128]{2,0,1:T(8,128)S(1)}, /*index=5*/f...) while((s32[]{:T(128)}, f32[16,3,128]{2,0,1:T(8,128)S(1)}, ...), condition=%wide.region_4.5_spmd.clone, body=%wide.region_0.4_spmd.clone.sunk | while | flops 6891705 | bytes 6684707 | solution.py:74
  156.4 1.4 compare_and_fusion.3
  166.4 1.4 compare_and_fusion.3
  176.3 1.4 compare_and_fusion.3
  186.3 1.4 compare_and_fusion.3
  196.2 1.4 compare_and_fusion.3
  206.1 1.4 compare_and_fusion.3
  216.1 1.4 compare_and_fusion.3
  226.0 1.4 compare_and_fusion.3
  235.9 1.4 compare_and_fusion.3
  245.9 1.4 compare_and_fusion.3
  255.8 1.4 compare_and_fusion.3
  265.7 1.4 compare_and_fusion.3
  275.7 1.4 compare_and_fusion.3
  285.6 1.4 compare_and_fusion.3
  295.6 1.4 compare_and_fusion.3
  305.5 1.4 compare_and_fusion.3
  310.7 1.7 reshape.157
  (327 shorter events, 111.5 us)
Async XLA Ops:
  0.0 315.1 %copy-start = (bf16[4,512,512]{2,1,0:T(8,128)(2,1)S(1)}, bf16[4,512,512]{2,1,0:T(8,128)(2,1)}, u32[]{:S(2)}) copy-start(bf16[4,512,512]{2,1,0:T(8,128)(2,1)} %param.21) | copy-start | bytes 6291460
  1.8 149.8 %collective-permute-start = (bf16[6,16,128]{2,1,0:T(8,128)(2,1)S(1)}, bf16[6,16,128]{2,1,0:T(8,128)(2,1)S(1)}, u32[]{:S(2)}, u32[]{:S(2)}) collective-permute-start(bf16[6,16,128]{2,1,0:T(8,128)(2,1)S(1)} %pad_maximum_fusion), channel_id=1, source_target_pairs={{0,1},{1,2},{2,3},{3,4},{4,5},{5,6},{6,7},{7,8},{8,9},{9,10},{10,1... | collective-permute-start | bytes 73736 | tf_op jit(solution)/shard_map/ppermute | solution.py:28
  5.7 145.9 %collective-permute-start.1 = (bf16[6,16,128]{2,1,0:T(8,128)(2,1)S(1)}, bf16[6,16,128]{2,1,0:T(8,128)(2,1)S(1)}, u32[]{:S(2)}, u32[]{:S(2)}) collective-permute-start(bf16[6,16,128]{2,1,0:T(8,128)(2,1)S(1)} %pad_maximum_fusion), channel_id=1, source_target_pairs={{1,0},{2,1},{3,2},{4,3},{5,4},{6,5},{7,6},{8,7},{9,8},{10,9},{11,1... | collective-permute-start | bytes 73736 | tf_op jit(solution)/shard_map/ppermute | solution.py:29
  11.3 139.0 %copy-start.2 = (s32[1,189]{1,0:T(1,128)S(1)}, s32[1,189]{1,0:T(1,128)}, u32[]{:S(2)}) copy-start(s32[1,189]{1,0:T(1,128)} %param.17) | copy-start | bytes 2272
  11.8 139.9 %copy-start.4 = (s32[16]{0:T(128)S(1)}, s32[16]{0:T(128)}, u32[]{:S(2)}) copy-start(s32[16]{0:T(128)} %param.16) | copy-start | bytes 196
  18.4 292.3 %all-to-all-start = ((bf16[512,2,256]{2,1,0:T(2,128)(2,1)}), bf16[512,2,256]{2,1,0:T(2,128)(2,1)S(1)}, u32[]{:S(2)}, u32[]{:S(2)}) async-start(bf16[512,2,256]{2,1,0:T(2,128)(2,1)} %reshape.156), calls=%async_computation | async-start | bytes 1048576 | tf_op jit(solution)/shard_map/all_to_all | solution.py:11
  310.7 4.1 %copy-start.3 = (s32[1,189]{1,0:T(1,128)S(1)}, s32[1,189]{1,0:T(1,128)}, u32[]{:S(2)}) copy-start(s32[1,189]{1,0:T(1,128)} %param.18) | copy-start | bytes 2272
  313.8 1.9 copy-start.1
